TPU v7x, 32 devices: a whole 2x2x4 slice. The times are simulated.
32 devices in a mesh: ri: 2 (over y), mu: 4 (over x, core), nu: 4 (over z).
Axes of the slice: x: 2, y: 2, z: 4, core: 2. Of those that a mesh axis runs over, the one named last changes fastest.
Arguments:
- three_center: bfloat16 [8, 2304, 128, 128], P('ri', ('mu', 'nu')), may hold values from -0.15625 to 0.15625
- block_pairs: int32 [2304, 2], P(('mu', 'nu')), may hold values from -1 to 95, as said below
- occ_factor: bfloat16 [12288, 128], P(('mu', 'nu')), may hold values from -6 to 6
- virt_density: bfloat16 [12288, 12288], P(('mu', 'nu'), 'ri'), may hold values from -0.0546875 to 0.0546875
- block_sizes: int32 [96], replicated, may hold values from 96 to 128
- occ_mask: int32 [96], replicated, may hold values 0 or 1
- virt_mask: int32 [96, 96], replicated, may hold values 0 or 1
Outputs:
- transformed: bfloat16 [8, 12288, 128], P('ri', ('mu', 'nu'))
Inputs may be any that keep to these rules, and one draw needn't show every extreme that they name: `block_pairs`: slots k in [d * 144, (d + 1) * 144) belong to device d of mu+nu; a live slot holds a mu block of that device's mu range (the range of 24 blocks of its mu index) and any nu block; empty slots hold -1 in both columns, and the live slots of a device come first. Every mu block appears in exactly 12 live slots, with distinct nu blocks. A device holds at most 144 live slots, and in every mu range some device holds exactly 144.
All inputs are finite; a program needn't handle non-finite values.
Results may differ from a plain program's by a relative error of at most 0.015.
Values may be sent and summed in bfloat16 or wider, within the bound.
No kernel may reach another device: no remote copies, remote signals or barrier semaphores. Data moves between devices by JAX's collectives and lax.ppermute only.
A program may use at most 192 MiB of HBM per device.

v0:
```python
import jax
import jax.numpy as jnp
from jax import lax
from jax.sharding import PartitionSpec as P

BS = 128
NB = 96


def body(three_center, block_pairs, occ_factor, virt_density, block_sizes, occ_mask, virt_mask):
    rows_dev = virt_density.shape[0]
    occ_cols = occ_factor.shape[1]
    ri_rows = three_center.shape[0]
    blocks_mu = NB // lax.axis_size("mu")
    total_rows = NB * BS
    inside = jnp.arange(BS, dtype=jnp.int32)[None, :] < block_sizes[:, None]
    keep_occ = (inside & (occ_mask[:, None] > 0)).reshape(total_rows)
    gathered_occ = lax.all_gather(occ_factor, ("mu", "nu"), axis=0, tiled=True)
    occ_kept = jnp.where(keep_occ[:, None], gathered_occ, jnp.zeros((), jnp.bfloat16))
    mu_block = block_pairs[:, 0]
    nu_block = jnp.clip(block_pairs[:, 1], 0, NB - 1)
    slot_live = mu_block >= 0
    occ_blocks = occ_kept.reshape(NB, BS, occ_cols)[nu_block]
    products = jnp.einsum(
        "pkab,kbo->pkao", three_center, occ_blocks, preferred_element_type=jnp.float32
    )
    local_block = mu_block - lax.axis_index("mu") * blocks_mu
    segment_ids = jnp.where(slot_live, local_block, blocks_mu)

    def slot_sum(slab_products):
        return jax.ops.segment_sum(slab_products, segment_ids, num_segments=blocks_mu + 1)[
            :blocks_mu
        ]

    partial_value = jax.vmap(slot_sum)(products)
    partial_value = partial_value.reshape(ri_rows, blocks_mu * BS, occ_cols)
    virt_all = lax.all_gather(virt_density, "ri", axis=1, tiled=True)
    row_start = (lax.axis_index("mu") * lax.axis_size("nu") + lax.axis_index("nu")) * rows_dev
    row_ids = row_start + jnp.arange(rows_dev, dtype=jnp.int32)
    block_pick = (row_ids[:, None] // BS == jnp.arange(NB, dtype=jnp.int32)[None, :]).astype(
        jnp.float32
    )
    mask_rows = jnp.dot(block_pick, virt_mask.astype(jnp.float32)) > 0.5
    row_inside = lax.dynamic_slice_in_dim(inside.reshape(total_rows), row_start, rows_dev)
    keep_virt = (mask_rows[:, :, None] & inside[None, :, :] & row_inside[:, None, None]).reshape(
        rows_dev, total_rows
    )
    virt_kept = jnp.where(keep_virt, virt_all, jnp.zeros((), jnp.bfloat16))
    summed = lax.psum(partial_value.astype(jnp.bfloat16), "nu")
    result = jnp.einsum(
        "sm,pmo->pso",
        virt_kept,
        lax.all_gather(summed, "mu", axis=1, tiled=True),
        preferred_element_type=jnp.float32,
    )
    return result.astype(jnp.bfloat16)


def solution(mesh):
    in_specs = (
        P("ri", ("mu", "nu"), None, None),
        P(("mu", "nu"), None),
        P(("mu", "nu"), None),
        P(("mu", "nu"), "ri"),
        P(),
        P(),
        P(),
    )
    out_specs = P("ri", ("mu", "nu"), None)
    return jax.shard_map(body, mesh=mesh, in_specs=in_specs, out_specs=out_specs, check_vma=False)
```

profile of v0, /device:TPU:0, one launch (start us, length us, event | category | flops | bytes accessed | tf_op | source)
XLA Modules:
  0.0 576.3 jit_solution(4603569849631304014)
XLA Ops:
  7.4 0.0 all-gather.4.cloned.1.call-start
  7.4 0.7 all-gather.4.cloned.1.call-update
  8.1 0.0 all-reduce.2.cloned.1.call-start
  8.1 0.8 compare_select_fusion
  8.9 0.7 broadcast_compare_fusion
  9.6 0.7 bitcast_compare_fusion
  10.3 48.4 %all-gather.4.cloned.1.call-done = bf16[12288,128]{1,0:T(8,128)(2,1)} async-done(((bf16[768,128]{1,0:T(8,128)(2,1)}), bf16[12288,128]{1,0:T(8,128)(2,1)}) %all-gather.4.cloned.1.call-update) | async-done | bytes 3145744 | tf_op jit(solution)/shard_map/all_gather | solution.py:18
  58.7 8.4 %broadcast_select_fusion = bf16[12288,128]{1,0:T(8,128)(2,1)S(1)} fusion(bf16[12288,128]{1,0:T(8,128)(2,1)} %all-gather.4.cloned.1.call-done, pred[12288]{0:T(1024)(128)(4,1)S(1)} %get-tuple-element.8), kind=kLoop, calls=%fused_computation.15 | loop fusion | flops 1572864 | bytes 6303744 | tf_op jit(solution)/shard_map/jit(_where)/select_n | solution.py:19
  67.1 7.5 %gather_fusion = bf16[144,128,128]{2,1,0:T(8,128)(2,1)} fusion(bf16[96,128,128]{2,1,0:T(8,128)(2,1)S(1)} %bitcast.47, s32[1024]{0:T(1024)S(1)} %pad_clamp_fusion), kind=kCustom, calls=%fused_computation | custom fusion | bytes 9437760 | tf_op jit(solution)/shard_map/gather | solution.py:23
  74.7 20.3 %fusion.9 = f32[144,4,128,128]{2,3,1,0:T(8,128)} fusion(bf16[4,144,128,128]{3,2,1,0:T(8,128)(2,1)} %param.7, bf16[144,128,128]{2,1,0:T(8,128)(2,1)} %gather_fusion), kind=kOutput, calls=%fused_computation.11 | convolution fusion | flops 2415919104 | bytes 61341696 | tf_op jit(solution)/shard_map/pkab,kbo->pkao/dot_general | solution.py:24
  95.0 36.8 %copy.13 = f32[144,4,128,128]{3,2,1,0:T(8,128)} copy(f32[144,4,128,128]{2,3,1,0:T(8,128)} %fusion.9) | data formatting | bytes 75497472 | tf_op jit(solution)/shard_map/pkab,kbo->pkao/transpose | solution.py:24
  131.8 3.5 broadcast_in_dim.21
  135.3 80.8 %scatter_fusion = f32[4,25,128,128]{3,2,1,0:T(8,128)} fusion(f32[4,25,128,128]{3,2,1,0:T(8,128)} %broadcast_in_dim.21, s32[144]{0:T(256)S(1)} %bitcast.52, f32[144,4,128,128]{3,2,1,0:T(8,128)} %copy.13), kind=kCustom, calls=%fused_computation.1 | custom fusion | flops 9437184 | bytes 113246784 | tf_op jit(solution)/shard_map/vmap()/scatter-add | solution.py:31
  216.1 3.5 slice.19
  219.6 2.8 copy.20
  222.4 0.0 all-reduce.2.cloned.1.call-update
  222.4 0.0 all-gather.8.cloned.1.call-start
  222.5 0.5 all-gather.8.cloned.1.call-update
  223.0 0.2 all-gather.6.cloned.1.call-start
  223.2 120.3 %all-reduce.2.cloned.1.call-done = bf16[4,3072,128]{1,2,0:T(8,128)(2,1)} async-done(((bf16[4,3072,128]{1,2,0:T(8,128)(2,1)}), bf16[4,3072,128]{1,2,0:T(8,128)(2,1)}) %all-reduce.2.cloned.1.call-update) | async-done | bytes 3145744 | tf_op jit(solution)/shard_map/psum | solution.py:49
  343.5 0.0 all-gather.6.cloned.1.call-update
  343.5 0.0 copy-done.1
  343.5 0.3 convolution_compare_fusion
  343.9 0.2 copy.15
  344.1 0.1 dynamic_slice.3
  344.2 0.0 copy-done
  344.2 0.2 lt.49
  344.4 104.0 %all-gather.8.cloned.1.call-done = bf16[768,12288]{1,0:T(8,128)(2,1)} async-done(((bf16[768,6144]{1,0:T(8,128)(2,1)}), bf16[768,12288]{1,0:T(8,128)(2,1)}) %all-gather.8.cloned.1.call-update) | async-done | bytes 18874384 | tf_op jit(solution)/shard_map/all_gather | solution.py:37
  448.4 83.4 %all-gather.6.cloned.1.call-done = bf16[4,12288,128]{1,2,0:T(8,128)(2,1)} async-done(((bf16[4,3072,128]{1,2,0:T(8,128)(2,1)}), bf16[4,12288,128]{1,2,0:T(8,128)(2,1)}) %all-gather.6.cloned.1.call-update) | async-done | bytes 12582928 | tf_op jit(solution)/shard_map/all_gather | solution.py:53
  531.8 13.5 %and.60 = pred[768,96,128]{2,1,0:T(32,128)(4,1)} broadcast(pred[768,96]{1,0:T(8,128)(4,1)S(1)} %copy.15), dimensions={0,1} | broadcast | bytes 9510912 | tf_op jit(solution)/shard_map/and | solution.py:45
  545.3 22.4 %fusion.17 = bf16[4,768,128]{1,2,0:T(8,128)(2,1)S(1)} fusion(bf16[4,12288,128]{1,2,0:T(8,128)(2,1)} %all-gather.6.cloned.1.call-done, bf16[768,12288]{1,0:T(8,128)(2,1)} %all-gather.8.cloned.1.call-done, pred[96,8,96,128]{3,2,1,0:T(32,128)(4,1)} %bitcast.49, pred[768]{0:T(1024)(128)(4,1)S(1)} %dynamic_slice.3, pred[12288]{0:T(1024)(128)(4,1)S(1)} %bitcast_compare_fusion.1), kind=kOutput, calls=%fused_computation.17 | convolution fusion | flops 9692381184 | bytes 41693952 | tf_op jit(solution)/shard_map/sm,pmo->pso/dot_general | solution.py:50
  567.7 1.2 copy.16
  (5 shorter events, 0.0 us)
Async XLA Ops:
  7.4 51.3 %all-gather.4.cloned.1.call-start = ((), (), s32[]{:S(2)}) async-start(), calls=%async_computation | async-start | bytes 3342336 | tf_op jit(solution)/shard_map/all_gather | solution.py:18
  8.1 335.4 %all-reduce.2.cloned.1.call-start = ((), (), s32[]{:S(2)}) async-start(), calls=%async_computation.1 | async-start | bytes 6291456 | tf_op jit(solution)/shard_map/psum | solution.py:49
  222.4 121.2 %copy-start.1 = (s32[96,96]{1,0:T(8,128)S(1)}, s32[96,96]{1,0:T(8,128)}, u32[]{:S(2)}) copy-start(s32[96,96]{1,0:T(8,128)} %param.13) | copy-start | bytes 110596
  222.4 121.8 %copy-start = (s32[96]{0:T(128)S(1)}, s32[96]{0:T(128)}, u32[]{:S(2)}) copy-start(s32[96]{0:T(128)} %param.11) | copy-start | bytes 1156
  222.4 226.0 %all-gather.8.cloned.1.call-start = ((), (), s32[]{:S(2)}) async-start(), calls=%async_computation.3 | async-start | bytes 28311552 | tf_op jit(solution)/shard_map/all_gather | solution.py:37
  223.0 308.8 %all-gather.6.cloned.1.call-start = ((), (), s32[]{:S(2)}) async-start(), calls=%async_computation.2 | async-start | bytes 15728640 | tf_op jit(solution)/shard_map/all_gather | solution.py:53
Sparse Core Ops, SparseCore 0:
  10.5 48.1 all-gather.3
  222.5 120.9 all-reduce.1
Sparse Core Ops, SparseCore 1:
  224.5 223.9 all-gather.7
  449.9 81.9 all-gather.5
where the time goes:
time: 577 us; the launch traced here: 576 us
  waiting for transfers between devices  357 us (62%)
  other arithmetic  91.5 us (16%)
  local copies, waits for them, and re-layouts  69.3 us (12%)
  matrix products  43 us (7%)
  between operations  14.9 us (3%)
    psum x1, waiting for transfers between devices, body(): summed = lax.psum(partial_value.astype(jnp.bfloat16), 'nu')  120 us
    all_gather x1, waiting for transfers between devices, body(): virt_all = lax.all_gather(virt_density, 'ri', axis=1, tiled=True)  104 us
    all_gather x1, waiting for transfers between devices, body(): lax.all_gather(summed, 'mu', axis=1, tiled=True)  83.4 us
    scatter-add x1, other arithmetic, slot_sum(): jax.ops.segment_sum(slab_products, segment_ids, num_segments=blocks_mu + 1)  80.8 us
    all_gather x1, waiting for transfers between devices, body(): gathered_occ = lax.all_gather(occ_factor, ('mu', 'nu'), axis=0, tiled=True)  48.4 us
    transpose x1, local copies, waits for them, and re-layouts, body(): jnp.einsum('pkab,kbo->pkao', three_center, occ_blocks, preferred_element_...  36.8 us
    dot_general x1, matrix products, body(): jnp.einsum('sm,pmo->pso', virt_kept, lax.all_gather(summed, 'mu', axis=1,...  22.4 us
    dot_general x1, matrix products, body(): jnp.einsum('pkab,kbo->pkao', three_center, occ_blocks, preferred_element_...  20.3 us
  transfers between devices with their start and end apart: 4, of which 4 were waited for; matrix products, arithmetic and copies ran while one was open for 1% of the time, Pallas kernels for 0%

commit v1 on v0

--- a/solution.py
+++ b/solution.py
@@ -46,7 +46,7 @@
         rows_dev, total_rows
     )
     virt_kept = jnp.where(keep_virt, virt_all, jnp.zeros((), jnp.bfloat16))
-    summed = lax.psum(partial_value.astype(jnp.bfloat16), "nu")
+    summed = jnp.sum(lax.all_gather(partial_value.astype(jnp.bfloat16), "nu"), axis=0)
     result = jnp.einsum(
         "sm,pmo->pso",
         virt_kept,

time: 577 us -> 791 us (1.37)
  waiting for transfers between devices: 357 us -> 564 us
    all_gather x0 -> x1, waiting for transfers between devices: none -> 217 us  [body(): lax.all_gather(partial_value.astype(jnp.bfloat16), 'nu')]
    psum x1 -> x0, waiting for transfers between devices: 120 us -> none  [body(): summed = lax.psum(partial_value.astype(jnp.bfloat16), 'nu')]
    all_gather x1, waiting for transfers between devices: 104 us -> 213 us  [body(): virt_all = lax.all_gather(virt_density, 'ri', axis=1, tiled=True)]
  transfers between devices with their start and end apart: 4 -> 4, of which waited for: 4 -> 4; matrix products, arithmetic and copies ran while one was open for 1% -> 2% of each run, Pallas kernels for 0% -> 0%
where the time goes in v1:
time: 791 us; the launch traced here: 790 us
  waiting for transfers between devices  564 us (71%)
  other arithmetic  98.4 us (12%)
  local copies, waits for them, and re-layouts  71 us (9%)
  matrix products  43 us (5%)
  between operations  13.2 us (2%)
    all_gather x1, waiting for transfers between devices, body(): lax.all_gather(partial_value.astype(jnp.bfloat16), 'nu')  217 us
    all_gather x1, waiting for transfers between devices, body(): virt_all = lax.all_gather(virt_density, 'ri', axis=1, tiled=True)  213 us
    all_gather x1, waiting for transfers between devices, body(): lax.all_gather(summed, 'mu', axis=1, tiled=True)  83.5 us
    scatter-add x1, other arithmetic, slot_sum(): jax.ops.segment_sum(slab_products, segment_ids, num_segments=blocks_mu + 1)  80.8 us
    all_gather x1, waiting for transfers between devices, body(): gathered_occ = lax.all_gather(occ_factor, ('mu', 'nu'), axis=0, tiled=True)  48.4 us
    transpose x1, local copies, waits for them, and re-layouts, body(): jnp.einsum('pkab,kbo->pkao', three_center, occ_blocks, preferred_element_...  36.8 us
    dot_general x1, matrix products, body(): jnp.einsum('sm,pmo->pso', virt_kept, lax.all_gather(summed, 'mu', axis=1,...  22.4 us
    dot_general x1, matrix products, body(): jnp.einsum('pkab,kbo->pkao', three_center, occ_blocks, preferred_element_...  20.3 us
  transfers between devices with their start and end apart: 4, of which 4 were waited for; matrix products, arithmetic and copies ran while one was open for 2% of the time, Pallas kernels for 0%

profile of v1, /device:TPU:0, one launch (start us, length us, event | category | flops | bytes accessed | tf_op | source)
XLA Modules:
  0.0 789.7 jit_solution(10363701335061532664)
XLA Ops:
  6.5 0.7 all-gather.5.cloned.1.call-update
  7.3 0.0 all-gather.7.cloned.1.call-start
  7.3 0.8 compare_select_fusion
  8.1 0.7 broadcast_compare_fusion
  8.7 0.7 bitcast_compare_fusion
  9.5 48.4 %all-gather.5.cloned.1.call-done = bf16[12288,128]{1,0:T(8,128)(2,1)} async-done(((bf16[768,128]{1,0:T(8,128)(2,1)}), bf16[12288,128]{1,0:T(8,128)(2,1)}) %all-gather.5.cloned.1.call-update) | async-done | bytes 3145744 | tf_op jit(solution)/shard_map/all_gather | solution.py:18
  57.9 8.4 %broadcast_select_fusion = bf16[12288,128]{1,0:T(8,128)(2,1)S(1)} fusion(bf16[12288,128]{1,0:T(8,128)(2,1)} %all-gather.5.cloned.1.call-done, pred[12288]{0:T(1024)(128)(4,1)S(1)} %get-tuple-element.8), kind=kLoop, calls=%fused_computation.15 | loop fusion | flops 1572864 | bytes 6303744 | tf_op jit(solution)/shard_map/jit(_where)/select_n | solution.py:19
  66.3 7.5 gather_fusion
  73.9 20.3 %fusion.9 = f32[144,4,128,128]{2,3,1,0:T(8,128)} fusion(bf16[4,144,128,128]{3,2,1,0:T(8,128)(2,1)} %param.7, bf16[144,128,128]{2,1,0:T(8,128)(2,1)} %gather_fusion), kind=kOutput, calls=%fused_computation.11 | convolution fusion | flops 2415919104 | bytes 61341696 | tf_op jit(solution)/shard_map/pkab,kbo->pkao/dot_general | solution.py:24
  94.1 36.8 %copy.18 = f32[144,4,128,128]{3,2,1,0:T(8,128)} copy(f32[144,4,128,128]{2,3,1,0:T(8,128)} %fusion.9) | data formatting | bytes 75497472 | tf_op jit(solution)/shard_map/pkab,kbo->pkao/transpose | solution.py:24
  131.0 3.5 broadcast_in_dim.21
  134.5 80.8 %scatter_fusion = f32[4,25,128,128]{3,2,1,0:T(8,128)} fusion(f32[4,25,128,128]{3,2,1,0:T(8,128)} %broadcast_in_dim.21, s32[144]{0:T(256)S(1)} %bitcast.52, f32[144,4,128,128]{3,2,1,0:T(8,128)} %copy.18), kind=kCustom, calls=%fused_computation.1 | custom fusion | flops 9437184 | bytes 113246784 | tf_op jit(solution)/shard_map/vmap()/scatter-add | solution.py:31
  215.3 5.1 slice.19
  220.4 0.0 all-gather.7.cloned.1.call-update
  220.4 0.0 all-gather.11.cloned.1.call-start
  220.5 0.7 all-gather.11.cloned.1.call-update
  221.2 0.0 copy-start.1
  221.2 0.0 copy-start
  221.2 0.2 all-gather.9.cloned.1.call-start
  221.4 217.2 %all-gather.7.cloned.1.call-done = bf16[4,4,3072,128]{3,2,1,0:T(8,128)(2,1)} async-done(((bf16[1,4,3072,128]{3,2,1,0:T(8,128)(2,1)}), bf16[4,4,3072,128]{3,2,1,0:T(8,128)(2,1)}) %all-gather.7.cloned.1.call-update) | async-done | bytes 12582928 | tf_op jit(solution)/shard_map/all_gather | solution.py:49
  438.6 6.9 reduce_sum.12
  445.6 2.8 copy.19
  448.4 0.0 all-gather.9.cloned.1.call-update
  448.5 0.3 convolution_compare_fusion
  448.8 0.2 copy.20
  449.0 0.1 dynamic_slice.3
  449.1 0.2 lt.49
  449.3 213.3 %all-gather.11.cloned.1.call-done = bf16[768,12288]{1,0:T(8,128)(2,1)} async-done(((bf16[768,6144]{1,0:T(8,128)(2,1)}), bf16[768,12288]{1,0:T(8,128)(2,1)}) %all-gather.11.cloned.1.call-update) | async-done | bytes 18874384 | tf_op jit(solution)/shard_map/all_gather | solution.py:37
  662.6 83.5 %all-gather.9.cloned.1.call-done = bf16[4,12288,128]{1,2,0:T(8,128)(2,1)} async-done(((bf16[4,3072,128]{1,2,0:T(8,128)(2,1)}), bf16[4,12288,128]{1,2,0:T(8,128)(2,1)}) %all-gather.9.cloned.1.call-update) | async-done | bytes 12582928 | tf_op jit(solution)/shard_map/all_gather | solution.py:53
  746.2 13.5 %and.60 = pred[768,96,128]{2,1,0:T(32,128)(4,1)} broadcast(pred[768,96]{1,0:T(8,128)(4,1)S(1)} %copy.20), dimensions={0,1} | broadcast | bytes 9510912 | tf_op jit(solution)/shard_map/and | solution.py:45
  759.7 22.4 %fusion.17 = bf16[4,768,128]{1,2,0:T(8,128)(2,1)S(1)} fusion(bf16[4,12288,128]{1,2,0:T(8,128)(2,1)} %all-gather.9.cloned.1.call-done, bf16[768,12288]{1,0:T(8,128)(2,1)} %all-gather.11.cloned.1.call-done, pred[96,8,96,128]{3,2,1,0:T(32,128)(4,1)} %bitcast.49, pred[768]{0:T(1024)(128)(4,1)S(1)} %dynamic_slice.3, pred[12288]{0:T(1024)(128)(4,1)S(1)} %bitcast_compare_fusion.1), kind=kOutput, calls=%fused_computation.17 | convolution fusion | flops 9692381184 | bytes 41693952 | tf_op jit(solution)/shard_map/sm,pmo->pso/dot_general | solution.py:50
  782.1 1.2 copy.21
  (6 shorter events, 0.0 us)
Async XLA Ops:
  6.5 51.3 %all-gather.5.cloned.1.call-start = ((), (), s32[]{:S(2)}) async-start(), calls=%async_computation | async-start | bytes 3342336 | tf_op jit(solution)/shard_map/all_gather | solution.py:18
  7.3 431.4 %all-gather.7.cloned.1.call-start = ((), (), s32[]{:S(2)}) async-start(), calls=%async_computation.1 | async-start | bytes 15728640 | tf_op jit(solution)/shard_map/all_gather | solution.py:49
  220.4 442.2 %all-gather.11.cloned.1.call-start = ((), (), s32[]{:S(2)}) async-start(), calls=%async_computation.3 | async-start | bytes 28311552 | tf_op jit(solution)/shard_map/all_gather | solution.py:37
  221.2 227.3 %copy-start.1 = (s32[96,96]{1,0:T(8,128)S(1)}, s32[96,96]{1,0:T(8,128)}, u32[]{:S(2)}) copy-start(s32[96,96]{1,0:T(8,128)} %param.13) | copy-start | bytes 110596
  221.2 228.0 %copy-start = (s32[96]{0:T(128)S(1)}, s32[96]{0:T(128)}, u32[]{:S(2)}) copy-start(s32[96]{0:T(128)} %param.11) | copy-start | bytes 1156
  221.2 525.0 %all-gather.9.cloned.1.call-start = ((), (), s32[]{:S(2)}) async-start(), calls=%async_computation.2 | async-start | bytes 15728640 | tf_op jit(solution)/shard_map/all_gather | solution.py:53
Sparse Core Ops, SparseCore 0:
  9.6 48.1 all-gather.4
  220.5 218.0 all-gather.6
  440.2 222.3 all-gather.10
  664.0 82.0 all-gather.8
